TPU v7x, 512 devices: a whole 4x8x8 slice. The times are simulated.
512 devices in a mesh: sub: 16 (over z, core), tile: 32 (over y, x).
Axes of the slice: x: 4, y: 8, z: 8, core: 2. Of those that a mesh axis runs over, the one named last changes fastest.
Arguments:
- echoes: float32 [32, 32, 128], P('sub', 'tile'), may hold values from -6 to 6
- pulse_offset: float32 [32, 32], P('sub', 'tile'), may hold values from 0 to 1
- range_gates: int32 [32, 32, 64], P('sub', 'tile'), may hold values from 0 to 511
- visible: int32 [32, 256], P('sub', 'tile'), may hold values 0 or 1
Outputs:
- images: float32 [32, 256, 128, 256], P('sub', 'tile')
- peak: float32 [256, 128, 128], P('tile', 'sub')
All inputs are finite; a program needn't handle non-finite values. No bound on the sum of `visible` on one device may be relied on, other than what follows from the above.
Results may differ from a plain program's by a relative error of at most 0.0037.
Values sent between devices are 32-bit elements; how exact they have to be, the bound alone decides.
No kernel may reach another device: no remote copies, remote signals or barrier semaphores. Data moves between devices by JAX's collectives and lax.ppermute only.
A program may use at most 64 MiB of HBM per device.

v0:
```python
import math
import jax
import jax.numpy as jnp
from jax import lax
from jax.sharding import PartitionSpec as P

PULSE_H = 32
FREQS = 64
PIX = 128
GATES = 512
grid_cols = 16
two_pi = 2.0 * math.pi


def shifted(block, axis, distance):
    devices = range(lax.axis_size(axis))
    route = [((i - distance) % len(devices), i) for i in devices]
    return lax.ppermute(block, axis, route)


def make_right(sine_wave):
    pixels = jnp.arange(PIX, dtype=jnp.float32)
    phase_grid = sine_wave[:, None] * pixels[None, :]
    real_part = jnp.cos(phase_grid).astype(jnp.bfloat16)
    imag_part = jnp.sin(phase_grid).astype(jnp.bfloat16)
    upper = jnp.concatenate([real_part, imag_part], axis=1)
    lower = jnp.concatenate([-imag_part, real_part], axis=1)
    return jnp.concatenate([upper, lower], axis=0)


def make_base(cosine_wave):
    pixels = jnp.arange(PIX, dtype=jnp.float32)
    base_phase = cosine_wave[None, :] * pixels[:, None]
    return (jnp.cos(base_phase), jnp.sin(base_phase))


def make_left(
    echo_real, echo_imag, cosine_wave, sine_wave, base_cos, base_sin, tile_number, norm_scale
):
    column = (tile_number % grid_cols * PIX - 8 * PIX).astype(jnp.float32)
    row_start = (tile_number // grid_cols * PIX - 4 * PIX).astype(jnp.float32)
    offset_phase = cosine_wave * column + sine_wave * row_start
    offset_cos = jnp.cos(offset_phase)
    offset_sin = jnp.sin(offset_phase)
    turned_real = norm_scale * (echo_real * offset_cos - echo_imag * offset_sin)
    turned_imag = norm_scale * (echo_real * offset_sin + echo_imag * offset_cos)
    real_part = turned_real[None, :] * base_cos - turned_imag[None, :] * base_sin
    imag_part = turned_real[None, :] * base_sin + turned_imag[None, :] * base_cos
    return jnp.concatenate([real_part, imag_part], axis=1).astype(jnp.bfloat16)


def on_device(echoes, pulse_offset, range_gates, visible):
    half_dev = echoes.shape[0]
    tile_dev = visible.shape[1]
    sub_count = lax.axis_size("sub")
    half_total = half_dev * sub_count
    first_half = lax.axis_index("sub") * half_dev
    first_tile = lax.axis_index("tile") * tile_dev
    half_numbers = first_half + jnp.arange(half_dev, dtype=jnp.int32)
    angles = two_pi * (half_numbers.astype(jnp.float32)[:, None] + pulse_offset) / half_total
    waves = 0.5 + range_gates.astype(jnp.float32) / GATES
    shown = visible.astype(jnp.float32)
    half_count = echoes.shape[0]
    norm_scale = (2.0 * PULSE_H * FREQS) ** (-0.5)
    echo_piece = lax.all_gather(echoes, "tile", axis=1, tiled=True)
    wave_piece = lax.all_gather(waves, "tile", axis=1, tiled=True)
    angle_piece = lax.all_gather(angles, "tile", axis=1, tiled=True)
    stacked = []
    for half_slot in range(half_count):
        cosine_wave = (wave_piece[half_slot] * jnp.cos(angle_piece[half_slot])[:, None]).reshape(-1)
        sine_wave = (wave_piece[half_slot] * jnp.sin(angle_piece[half_slot])[:, None]).reshape(-1)
        echo_real = echo_piece[half_slot][:, :FREQS].reshape(-1)
        echo_imag = echo_piece[half_slot][:, FREQS:].reshape(-1)
        right_side = make_right(sine_wave)
        base_cos, base_sin = make_base(cosine_wave)
        tile_terms = []
        for tile_slot in range(tile_dev):

            def compute(
                echo_real=echo_real,
                echo_imag=echo_imag,
                cosine_wave=cosine_wave,
                sine_wave=sine_wave,
                base_cos=base_cos,
                base_sin=base_sin,
                right_side=right_side,
                tile_slot=tile_slot,
            ):
                left_side = make_left(
                    echo_real,
                    echo_imag,
                    cosine_wave,
                    sine_wave,
                    base_cos,
                    base_sin,
                    first_tile + tile_slot,
                    norm_scale,
                )
                return jnp.dot(left_side, right_side, preferred_element_type=jnp.float32)

            tile_term = compute()
            tile_terms.append(tile_term)
        stacked.append(jnp.stack(tile_terms))
    half_images = jnp.stack(stacked)
    half_images = half_images * shown[:, :, None, None]
    following = shifted(half_images[0], "sub", -1)
    successors = jnp.concatenate([half_images[1:half_dev], following[None]], axis=0)
    images = half_images + successors
    power_map = images[..., :PIX] ** 2 + images[..., PIX:] ** 2
    local_peak = jnp.max(power_map, axis=0)
    full_peak = lax.pmax(local_peak, "sub")
    row_count = PIX // sub_count
    peak = lax.dynamic_slice_in_dim(full_peak, lax.axis_index("sub") * row_count, row_count, 1)
    return (images, peak)


def solution(mesh):
    in_specs = (P("sub", "tile", None), P("sub", "tile"), P("sub", "tile", None), P("sub", "tile"))
    out_specs = (P("sub", "tile", None, None), P("tile", "sub", None))
    return jax.shard_map(
        on_device, mesh=mesh, in_specs=in_specs, out_specs=out_specs, check_vma=False
    )
```

profile of v0, /device:TPU:1, one launch (start us, length us, event | category | flops | bytes accessed | tf_op | source)
XLA Modules:
  0.0 301.1 jit_solution(487523907034118992)
XLA Ops:
  7.3 0.7 multiply_bitcast_fusion
  8.0 29.8 %all-gather = f32[32,1,2]{2,1,0:T(1,128)S(1)} all-gather(f32[1,1,2]{2,1,0:T(1,128)S(1)} %multiply_bitcast_fusion), channel_id=1, replica_groups=mesh['sub'=16,'tile'=32] {'tile'}, dimensions={0}, use_global_device_ids=true | all-gather | bytes 264 | tf_op jit(solution)/shard_map/all_gather | solution.py:67
  37.8 0.1 copy.9
  37.9 0.1 mul.1893
  38.0 0.1 mul.1894
  38.1 0.1 mul.1901
  38.3 0.1 mul.2051
  38.4 0.1 mul.2055
  38.5 29.0 %all_gather.9 = f32[2,32,128]{2,0,1:T(2,128)S(1)} all-gather(f32[2,1,128]{2,0,1:T(2,128)} %bitcast.94), channel_id=1, replica_groups=mesh['sub'=16,'tile'=32] {'tile'}, dimensions={1}, use_global_device_ids=true | all-gather | bytes 33792 | tf_op jit(solution)/shard_map/all_gather | solution.py:65
  67.5 0.1 fusion.122
  67.7 0.1 fusion.123
  67.9 0.7 multiply_add_fusion.16
  68.6 28.6 %all_gather.10 = f32[2,32,64]{2,0,1:T(2,128)S(1)} all-gather(f32[2,1,64]{2,0,1:T(2,128)S(1)} %multiply_add_fusion.16), channel_id=1, replica_groups=mesh['sub'=16,'tile'=32] {'tile'}, dimensions={1}, use_global_device_ids=true | all-gather | bytes 16896 | tf_op jit(solution)/shard_map/all_gather | solution.py:66
  97.2 0.1 slice_reduce_fusion.1
  97.3 0.1 squeeze.11
  97.4 0.1 subtract_multiply_fusion
  97.5 4.5 %sine_convert_fusion.1 = (bf16[2048,128]{1,0:T(8,128)(2,1)S(1)}, bf16[2048,128]{1,0:T(8,128)(2,1)S(1)}) fusion(f32[2048]{0:T(1024)S(1)} %get-tuple-element.117), kind=kLoop, calls=%fused_computation.125 | loop fusion | flops 786432 | bytes 1056768 | tf_op jit(solution)/shard_map/convert_element_type | solution.py:25
  102.0 4.1 %fusion.70 = bf16[2048,128]{1,0:T(8,128)(2,1)S(1)} fusion(f32[2048]{0:T(1024)S(1)} %get-tuple-element.117), kind=kLoop, calls=%fused_computation.133 | loop fusion | flops 1310720 | bytes 532480 | tf_op jit(solution)/shard_map/neg | solution.py:27
  106.3 0.3 add_multiply_fusion.8
  106.6 0.3 add_multiply_fusion
  106.8 4.5 %sine_convert_fusion = (bf16[2048,128]{1,0:T(8,128)(2,1)S(1)}, bf16[2048,128]{1,0:T(8,128)(2,1)S(1)}) fusion(f32[2048]{0:T(1024)S(1)} %get-tuple-element.9), kind=kLoop, calls=%fused_computation.103 | loop fusion | flops 786432 | bytes 1056768 | tf_op jit(solution)/shard_map/convert_element_type | solution.py:25
  111.3 4.1 %fusion.71 = bf16[2048,128]{1,0:T(8,128)(2,1)S(1)} fusion(f32[2048]{0:T(1024)S(1)} %get-tuple-element.9), kind=kLoop, calls=%fused_computation.134 | loop fusion | flops 1310720 | bytes 532480 | tf_op jit(solution)/shard_map/neg | solution.py:27
  115.4 6.3 %subtract_convert_fusion.8 = (bf16[128,2048]{1,0:T(8,128)(2,1)S(1)}, bf16[128,2048]{1,0:T(8,128)(2,1)S(1)}, bf16[128,2048]{1,0:T(8,128)(2,1)S(1)}, bf16[128,2048...) fusion(f32[2048]{0:T(1024)S(1)} %get-tuple-element.12, ...), kind=kLoop, calls=%fused_computation.112 | loop fusion | flops 17039360 | bytes 8527872 | tf_op jit(solution)/shard_map/convert.16
  121.7 0.5 fusion.15
  122.2 0.5 fusion.14
  122.6 0.5 fusion.13
  123.1 0.5 fusion.12
  123.6 0.5 fusion.11
  124.1 0.5 fusion.10
  124.6 0.5 fusion.9
  125.1 0.5 fusion.8
  125.6 6.2 %subtract_convert_fusion = (bf16[128,2048]{1,0:T(8,128)(2,1)S(1)}, bf16[128,2048]{1,0:T(8,128)(2,1)S(1)}, bf16[128,2048]{1,0:T(8,128)(2,1)S(1)}, bf16[128,2048]{...) fusion(f32[2048]{0:T(1024)S(1)} %get-tuple-element.29, ...), kind=kLoop, calls=%fused_computation.90 | loop fusion | flops 17039360 | bytes 8527872 | tf_op jit(solution)/shard_map/convert
  131.8 0.4 fusion.7
  132.2 0.4 fusion.6
  132.7 0.4 fusion.5
  133.1 0.4 fusion.4
  133.6 0.4 fusion.3
  134.0 0.5 fusion.2
  134.5 0.5 fusion.1
  135.0 0.5 fusion
  135.5 0.3 maximum_multiply_fusion
  135.7 0.2 fusion.120
  135.9 25.8 %collective-permute-start = (f32[8,128,256]{2,1,0:T(8,128)S(1)}, f32[8,128,256]{2,1,0:T(8,128)S(1)}, u32[]{:S(2)}, u32[]{:S(2)}) collective-permute-start(f32[8,128,256]{2,1,0:T(8,128)S(1)} %get-tuple-element.11), channel_id=1, source_target_pairs={{32,0},{64,32},{96,64},{128,96},{160,128},{192,160},{224,192},{256... | collective-permute-start | bytes 3145736 | tf_op jit(solution)/shard_map/ppermute | solution.py:18
  161.7 13.5 %collective-permute-done = f32[8,128,256]{2,1,0:T(8,128)S(1)} collective-permute-done((f32[8,128,256]{2,1,0:T(8,128)S(1)}, f32[8,128,256]{2,1,0:T(8,128)S(1)}, u32[]{:S(2)}, u32[]{:S(2)}) %collective-permute-start) | collective-permute-done | bytes 1048608 | tf_op jit(solution)/shard_map/ppermute | solution.py:18
  175.2 0.3 maximum_add_fusion
  175.6 1.1 fusion.17
  176.7 116.2 %all-reduce.2.cloned.1.call-done = f32[8,128,128]{2,1,0:T(8,128)} async-done(((f32[8,128,128]{2,1,0:T(8,128)}), f32[8,128,128]{2,1,0:T(8,128)}) %all-reduce.2.cloned.1.call-update) | async-done | bytes 524304 | tf_op jit(solution)/shard_map/pmax | solution.py:111
  292.9 1.4 constant_dynamic-slice_fusion
  (19 shorter events, 0.8 us)
Async XLA Ops:
  7.2 285.7 %all-reduce.2.cloned.1.call-start = ((), (), s32[]{:S(2)}) async-start(), calls=%async_computation | async-start | bytes 1048576 | tf_op jit(solution)/shard_map/pmax | solution.py:111
  67.7 47.7 %copy-start.1 = (s32[2,8]{1,0:T(2,128)S(1)}, s32[2,8]{1,0:T(2,128)}, u32[]{:S(2)}) copy-start(s32[2,8]{1,0:T(2,128)} %param.7) | copy-start | bytes 196
  135.9 39.3 %collective-permute-start = (f32[8,128,256]{2,1,0:T(8,128)S(1)}, f32[8,128,256]{2,1,0:T(8,128)S(1)}, u32[]{:S(2)}, u32[]{:S(2)}) collective-permute-start(f32[8,128,256]{2,1,0:T(8,128)S(1)} %get-tuple-element.11), channel_id=1, source_target_pairs={{32,0},{64,32},{96,64},{128,96},{160,128},{192,160},{224,192},{256... | collective-permute-start | bytes 3145736 | tf_op jit(solution)/shard_map/ppermute | solution.py:18
  175.6 118.7 %copy-start = (f32[2,8,128,256]{3,2,1,0:T(8,128)}, f32[2,8,128,256]{3,2,1,0:T(8,128)S(1)}, u32[]{:S(2)}) copy-start(f32[2,8,128,256]{3,2,1,0:T(8,128)S(1)} %maximum_add_fusion) | copy-start | bytes 6291460
Sparse Core Ops, SparseCore 0:
  176.8 116.0 all-reduce.1
where the time goes:
time: 301 us
  waiting for transfers between devices  130 us (43%)
  blocking collectives  87.4 us (29%)
  other arithmetic  33.3 us (11%)
  starting transfers between devices  25.8 us (9%)
  between operations  14.5 us (5%)
  matrix products  7.47 us (2%)
    pmax x1, waiting for transfers between devices, on_device(): full_peak = lax.pmax(local_peak, 'sub')  116 us
    all_gather x1, blocking collectives, on_device(): angle_piece = lax.all_gather(angles, 'tile', axis=1, tiled=True)  29.8 us
    all_gather x1, blocking collectives, on_device(): echo_piece = lax.all_gather(echoes, 'tile', axis=1, tiled=True)  29 us
    all_gather x1, blocking collectives, on_device(): wave_piece = lax.all_gather(waves, 'tile', axis=1, tiled=True)  28.6 us
    ppermute x1, starting transfers between devices, shifted(): return lax.ppermute(block, axis, route)  25.8 us
    ppermute x1, waiting for transfers between devices, shifted(): return lax.ppermute(block, axis, route)  13.5 us
    another operation x2, other arithmetic  12.5 us
    convert_element_type x2, other arithmetic, make_right(): imag_part = jnp.sin(phase_grid).astype(jnp.bfloat16)  8.92 us
  transfers between devices with their start and end apart: 2, of which 2 were waited for; matrix products, arithmetic and copies ran while one was open for 0% of the time, Pallas kernels for 0%

commit v1 on v0

--- a/solution.py
+++ b/solution.py
@@ -63,7 +63,9 @@
     half_count = echoes.shape[0]
     norm_scale = (2.0 * PULSE_H * FREQS) ** (-0.5)
     echo_piece = lax.all_gather(echoes, "tile", axis=1, tiled=True)
-    wave_piece = lax.all_gather(waves, "tile", axis=1, tiled=True)
+    wave_piece = jnp.concatenate(
+        lax.all_to_all(jnp.stack([waves] * lax.axis_size("tile")), "tile", 0, 0), axis=1
+    )
     angle_piece = lax.all_gather(angles, "tile", axis=1, tiled=True)
     stacked = []
     for half_slot in range(half_count):

time: 301 us -> 278 us (0.924)
  blocking collectives: 87.4 us -> 57.9 us
    all_gather x1 -> x0, blocking collectives: 28.6 us -> none  [on_device(): wave_piece = lax.all_gather(waves, 'tile', axis=1, tiled=True)]
    all_to_all x0 -> x1, starting transfers between devices: none -> 10.5 us  [on_device(): lax.all_to_all(jnp.stack([waves] * lax.axis_size('tile')), 'tile', 0, 0)]
    ppermute x1, starting transfers between devices: 25.8 us -> 16.7 us  [shifted(): return lax.ppermute(block, axis, route)]
    another operation x2 -> x3, other arithmetic: 12.5 us -> 13.3 us
  transfers between devices with their start and end apart: 2 -> 3, of which waited for: 2 -> 2; matrix products, arithmetic and copies ran while one was open for 0% -> 1% of each run, Pallas kernels for 0% -> 0%
where the time goes in v1:
time: 278 us
  waiting for transfers between devices  131 us (47%)
  blocking collectives  57.9 us (21%)
  other arithmetic  35.5 us (13%)
  starting transfers between devices  27.3 us (10%)
  between operations  14.4 us (5%)
  matrix products  7.69 us (3%)
  local copies, waits for them, and re-layouts  4.21 us (2%)
    pmax x1, waiting for transfers between devices, on_device(): full_peak = lax.pmax(local_peak, 'sub')  116 us
    all_gather x1, blocking collectives, on_device(): echo_piece = lax.all_gather(echoes, 'tile', axis=1, tiled=True)  29.1 us
    all_gather x1, blocking collectives, on_device(): angle_piece = lax.all_gather(angles, 'tile', axis=1, tiled=True)  28.8 us
    ppermute x1, starting transfers between devices, shifted(): return lax.ppermute(block, axis, route)  16.7 us
    ppermute x1, waiting for transfers between devices, shifted(): return lax.ppermute(block, axis, route)  14.5 us
    another operation x2, other arithmetic  12.6 us
    all_to_all x1, starting transfers between devices, on_device(): lax.all_to_all(jnp.stack([waves] * lax.axis_size('tile')), 'tile', 0, 0)  10.5 us
    convert_element_type x2, other arithmetic, make_right(): imag_part = jnp.sin(phase_grid).astype(jnp.bfloat16)  8.92 us
  transfers between devices with their start and end apart: 3, of which 2 were waited for; matrix products, arithmetic and copies ran while one was open for 1% of the time, Pallas kernels for 0%

profile of v1, /device:TPU:1, one launch (start us, length us, event | category | flops | bytes accessed | tf_op | source)
XLA Modules:
  0.0 277.8 jit_solution(16509153993474741502)
XLA Ops:
  7.2 0.7 multiply_add_fusion.16
  7.9 0.5 broadcast.438
  8.4 0.7 reduce.8
  9.1 0.7 reshape.993
  9.8 10.5 %all-to-all-start = ((f32[32,1,128]{2,1,0:T(1,128)}), f32[32,1,128]{2,1,0:T(1,128)S(1)}, u32[]{:S(2)}, u32[]{:S(2)}) async-start(f32[32,1,128]{2,1,0:T(1,128)} %reshape.993), calls=%async_computation | async-start | bytes 32768 | tf_op jit(solution)/shard_map/all_to_all | solution.py:67
  20.4 0.7 multiply_bitcast_fusion
  21.0 28.8 %all-gather = f32[32,1,2]{2,1,0:T(1,128)S(1)} all-gather(f32[1,1,2]{2,1,0:T(1,128)S(1)} %multiply_bitcast_fusion), channel_id=1, replica_groups=mesh['sub'=16,'tile'=32] {'tile'}, dimensions={0}, use_global_device_ids=true | all-gather | bytes 264 | tf_op jit(solution)/shard_map/all_gather | solution.py:69
  49.9 0.1 copy.8
  49.9 29.1 %all_gather.6 = f32[2,32,128]{2,0,1:T(2,128)S(1)} all-gather(f32[2,1,128]{2,0,1:T(2,128)} %bitcast.97), channel_id=1, replica_groups=mesh['sub'=16,'tile'=32] {'tile'}, dimensions={1}, use_global_device_ids=true | all-gather | bytes 33792 | tf_op jit(solution)/shard_map/all_gather | solution.py:65
  79.1 0.1 fusion.122
  79.4 0.1 mul.1894
  80.2 0.7 convert_element_type.130
  80.9 0.7 reduce.9
  81.6 0.1 reshape.994
  81.7 0.1 slice_reduce_fusion.1
  81.9 0.1 subtract_multiply_fusion
  82.0 4.5 %sine_convert_fusion.1 = (bf16[2048,128]{1,0:T(8,128)(2,1)S(1)}, bf16[2048,128]{1,0:T(8,128)(2,1)S(1)}) fusion(f32[2048]{0:T(1024)S(1)} %get-tuple-element.117), kind=kLoop, calls=%fused_computation.125 | loop fusion | flops 786432 | bytes 1056768 | tf_op jit(solution)/shard_map/convert_element_type | solution.py:25
  86.5 4.1 %fusion.70 = bf16[2048,128]{1,0:T(8,128)(2,1)S(1)} fusion(f32[2048]{0:T(1024)S(1)} %get-tuple-element.117), kind=kLoop, calls=%fused_computation.133 | loop fusion | flops 1310720 | bytes 532480 | tf_op jit(solution)/shard_map/neg | solution.py:27
  90.7 0.3 add_multiply_fusion.8
  91.0 0.3 add_multiply_fusion
  91.2 4.5 %sine_convert_fusion = (bf16[2048,128]{1,0:T(8,128)(2,1)S(1)}, bf16[2048,128]{1,0:T(8,128)(2,1)S(1)}) fusion(f32[2048]{0:T(1024)S(1)} %get-tuple-element.9), kind=kLoop, calls=%fused_computation.103 | loop fusion | flops 786432 | bytes 1056768 | tf_op jit(solution)/shard_map/convert_element_type | solution.py:25
  95.7 4.1 %fusion.71 = bf16[2048,128]{1,0:T(8,128)(2,1)S(1)} fusion(f32[2048]{0:T(1024)S(1)} %get-tuple-element.9), kind=kLoop, calls=%fused_computation.134 | loop fusion | flops 1310720 | bytes 532480 | tf_op jit(solution)/shard_map/neg | solution.py:27
  99.8 6.3 %subtract_convert_fusion.8 = (bf16[128,2048]{1,0:T(8,128)(2,1)S(1)}, bf16[128,2048]{1,0:T(8,128)(2,1)S(1)}, bf16[128,2048]{1,0:T(8,128)(2,1)S(1)}, bf16[128,2048...) fusion(f32[2048]{0:T(1024)S(1)} %get-tuple-element.12, ...), kind=kLoop, calls=%fused_computation.112 | loop fusion | flops 17039360 | bytes 8527872 | tf_op jit(solution)/shard_map/convert.16
  106.1 0.5 fusion.15
  106.6 0.5 fusion.14
  107.1 0.5 fusion.13
  107.6 0.5 fusion.12
  108.0 0.5 fusion.11
  108.5 0.5 fusion.10
  109.0 0.5 fusion.9
  109.5 0.5 fusion.8
  110.0 6.3 %subtract_convert_fusion = (bf16[128,2048]{1,0:T(8,128)(2,1)S(1)}, bf16[128,2048]{1,0:T(8,128)(2,1)S(1)}, bf16[128,2048]{1,0:T(8,128)(2,1)S(1)}, bf16[128,2048]{...) fusion(f32[2048]{0:T(1024)S(1)} %get-tuple-element.29, ...), kind=kLoop, calls=%fused_computation.90 | loop fusion | flops 17039360 | bytes 8527872 | tf_op jit(solution)/shard_map/convert
  116.3 0.5 fusion.7
  116.8 0.5 fusion.6
  117.3 0.5 fusion.5
  117.7 0.5 fusion.4
  118.2 0.5 fusion.3
  118.7 0.5 fusion.2
  119.2 0.5 fusion.1
  119.7 0.5 fusion
  120.2 0.3 maximum_multiply_fusion
  120.4 0.1 fusion.120
  120.6 16.7 %collective-permute-start = (f32[8,128,256]{2,1,0:T(8,128)S(1)}, f32[8,128,256]{2,1,0:T(8,128)S(1)}, u32[]{:S(2)}, u32[]{:S(2)}) collective-permute-start(f32[8,128,256]{2,1,0:T(8,128)S(1)} %get-tuple-element.11), channel_id=1, source_target_pairs={{32,0},{64,32},{96,64},{128,96},{160,128},{192,160},{224,192},{256... | collective-permute-start | bytes 3145736 | tf_op jit(solution)/shard_map/ppermute | solution.py:18
  137.3 14.5 %collective-permute-done = f32[8,128,256]{2,1,0:T(8,128)S(1)} collective-permute-done((f32[8,128,256]{2,1,0:T(8,128)S(1)}, f32[8,128,256]{2,1,0:T(8,128)S(1)}, u32[]{:S(2)}, u32[]{:S(2)}) %collective-permute-start) | collective-permute-done | bytes 1048608 | tf_op jit(solution)/shard_map/ppermute | solution.py:18
  151.8 0.3 maximum_add_fusion
  152.1 1.1 fusion.17
  153.3 116.3 %all-reduce.2.cloned.1.call-done = f32[8,128,128]{2,1,0:T(8,128)} async-done(((f32[8,128,128]{2,1,0:T(8,128)}), f32[8,128,128]{2,1,0:T(8,128)}) %all-reduce.2.cloned.1.call-update) | async-done | bytes 524304 | tf_op jit(solution)/shard_map/pmax | solution.py:113
  269.6 1.4 constant_dynamic-slice_fusion
  (24 shorter events, 1.3 us)
Async XLA Ops:
  9.8 71.1 %all-to-all-start = ((f32[32,1,128]{2,1,0:T(1,128)}), f32[32,1,128]{2,1,0:T(1,128)S(1)}, u32[]{:S(2)}, u32[]{:S(2)}) async-start(f32[32,1,128]{2,1,0:T(1,128)} %reshape.993), calls=%async_computation | async-start | bytes 32768 | tf_op jit(solution)/shard_map/all_to_all | solution.py:67
  20.3 249.3 %all-reduce.2.cloned.1.call-start = ((), (), s32[]{:S(2)}) async-start(), calls=%async_computation.1 | async-start | bytes 1048576 | tf_op jit(solution)/shard_map/pmax | solution.py:113
  120.6 31.2 %collective-permute-start = (f32[8,128,256]{2,1,0:T(8,128)S(1)}, f32[8,128,256]{2,1,0:T(8,128)S(1)}, u32[]{:S(2)}, u32[]{:S(2)}) collective-permute-start(f32[8,128,256]{2,1,0:T(8,128)S(1)} %get-tuple-element.11), channel_id=1, source_target_pairs={{32,0},{64,32},{96,64},{128,96},{160,128},{192,160},{224,192},{256... | collective-permute-start | bytes 3145736 | tf_op jit(solution)/shard_map/ppermute | solution.py:18
  152.1 118.8 %copy-start = (f32[2,8,128,256]{3,2,1,0:T(8,128)}, f32[2,8,128,256]{3,2,1,0:T(8,128)S(1)}, u32[]{:S(2)}) copy-start(f32[2,8,128,256]{3,2,1,0:T(8,128)S(1)} %maximum_add_fusion) | copy-start | bytes 6291460
Sparse Core Ops, SparseCore 0:
  153.4 116.1 all-reduce.1
